TPU v7x, 32 devices: a whole 2x2x4 slice. The times are simulated.
32 devices in a mesh: layer: 4 (over y, x), head: 4 (over z), qblk: 2 (over core).
Axes of the slice: x: 2, y: 2, z: 4, core: 2. Of those that a mesh axis runs over, the one named last changes fastest.
Arguments:
- inputs: bfloat16 [384, 5120], P(('layer', 'qblk')), may hold values from -6 to 6
- key_weight: bfloat16 [5120, 512], P(None, 'head'), may hold values from -0.078125 to 0.078125
- value_weight: bfloat16 [5120, 512], P(None, 'head'), may hold values from -0.078125 to 0.078125
- queries: bfloat16 [4, 384, 2560], P('layer', 'qblk', 'head'), may hold values from -192 to 192
- output_cotangent: bfloat16 [4, 384, 2560], P('layer', 'qblk', 'head'), may hold values from -6 to 6
- documents: int32 [384], replicated, may hold values from 0 to 5, never falling along the last dimension, each value on 1 to 192 neighbouring positions
Outputs:
- query_gradient: bfloat16 [4, 384, 2560], P('layer', 'qblk', 'head')
- input_gradient: bfloat16 [384, 5120], P(('layer', 'qblk'), 'head')
Inputs may be any that keep to these rules, and one draw needn't show every extreme that they name: `documents`: never falls along the sequence; every document has 1 to 192 positions, and one has exactly 192.
All inputs are finite; a program needn't handle non-finite values.
Results may differ from a plain program's by a relative error of at most 0.018.
The roundings to bfloat16 on the way count: a program that leaves them out, or rounds other values in their place, can miss the bound.
Values may be sent and summed in bfloat16 or wider, within the bound.
A program may use at most 64 MiB of HBM per device.

v0:
```python
import functools

import jax
import jax.numpy as jnp
from jax import lax
from jax.experimental import pallas as pl
from jax.experimental.pallas import tpu as pltpu
from jax.sharding import PartitionSpec as P

MESH = pl.DeviceIdType.MESH
NT = (((1,), (1,)), ((), ()))
TN = (((0,), (0,)), ((), ()))
F32 = jnp.float32
BF16 = jnp.bfloat16


def backward_kernel(
    sizes,
    x_hbm,
    wk_hbm,
    wv_hbm,
    q_hbm,
    g_hbm,
    docs_hbm,
    qg_ref,
    ig_ref,
    x_v,
    w_v,
    qf,
    gf,
    kv,
    kvf,
    st,
    dpt,
    ds16,
    sbuf,
    rbuf,
    zsend,
    zrecv,
    far_w,
    far_kv,
    own_kv,
    own_v,
    docs_ref,
    load_sem,
    ag_send,
    ag_recv,
    rs_send,
    rs_recv,
    z_send,
    z_recv,
    far_send,
    far_recv,
):
    L, H, Q, r, R, S, D, hd, G, chunks, kb, line = sizes
    n = L * Q
    scaling = hd ** (-0.5)
    span = S // 2
    ly = lax.axis_index("layer")
    hh = lax.axis_index("head")
    qb = lax.axis_index("qblk")
    me = ly * Q + qb

    def needed(owner, block):
        above = owner * r < (block + 1) * R
        below = (owner + 1) * r - 1 >= block * R - span + 1
        return jnp.logical_and(above, below)

    def place(peer):
        return (peer // Q, hh, lax.rem(peer, Q))

    if L == 4 and Q == 2:
        row, col = ly // 2, lax.rem(ly, 2)
        far_layer = (1 - row) * 2 + 1 - col
        next_layers = [row * 2 + 1 - col, (1 - row) * 2 + col]
        peers = [far_layer * Q + qb, far_layer * Q + 1 - qb]
        peers += [layer * Q + qb for layer in next_layers]
        peers += [layer * Q + 1 - qb for layer in next_layers]
        peers += [ly * Q + 1 - qb]
    else:
        peers = [lax.rem(me + o, n) for o in range(1, n)]
    heads = [lax.rem(hh + o, H) for o in range(1, H)]

    barrier = pltpu.get_barrier_semaphore()
    for other in heads:
        pl.semaphore_signal(barrier, inc=1, device_id=(ly, other, qb), device_id_type=MESH)
    for peer in peers:
        pl.semaphore_signal(barrier, inc=1, device_id=place(peer), device_id_type=MESH)

    step = D // chunks
    loads = [pltpu.make_async_copy(x_hbm, x_v, load_sem.at[0])]
    for c in range(chunks):
        rows = pl.ds(c * step, step)
        loads.append(
            pltpu.make_async_copy(
                wk_hbm.at[rows, :], w_v.at[rows, pl.ds(0, hd)], load_sem.at[1 + 2 * c]
            )
        )
        loads.append(
            pltpu.make_async_copy(
                wv_hbm.at[rows, :], w_v.at[rows, pl.ds(hd, hd)], load_sem.at[2 + 2 * c]
            )
        )
    base = 1 + 2 * chunks
    docs_load = pltpu.make_async_copy(docs_hbm, docs_ref, load_sem.at[base + 2 * G])
    docs_load.start()
    for g in range(G):
        cols = pl.ds(g * hd, hd)
        rows = pl.ds(g * R, R)
        loads.append(
            pltpu.make_async_copy(q_hbm.at[0, :, cols], qf.at[rows, :], load_sem.at[base + 2 * g])
        )
        loads.append(
            pltpu.make_async_copy(
                g_hbm.at[0, :, cols], gf.at[rows, :], load_sem.at[base + 2 * g + 1]
            )
        )
    for load in loads:
        load.start()

    loads[0].wait()
    acc = jnp.zeros((r, 2 * hd), F32)
    for c in range(chunks):
        loads[1 + 2 * c].wait()
        loads[2 + 2 * c].wait()
        acc = acc + jnp.dot(
            x_v[:, c * step : (c + 1) * step],
            w_v[c * step : (c + 1) * step, :],
            preferred_element_type=F32,
        )
    mine = acc.astype(BF16)
    for k in range(2):
        own_v[k] = mine[:, k * hd : (k + 1) * hd]
    pl.semaphore_wait(barrier, n - 1 + H - 1)

    def gather_copy(k, peer, slot):
        return pltpu.make_async_remote_copy(
            src_ref=own_v.at[k],
            dst_ref=kv.at[k, slot],
            send_sem=ag_send.at[k * n + peer],
            recv_sem=ag_recv.at[k * n + slot],
            device_id=place(peer),
            device_id_type=MESH,
        )

    for k in range(2):
        for peer in peers:

            @pl.when(needed(me, lax.rem(peer, Q)))
            def _(k=k, peer=peer):
                gather_copy(k, peer, me).start()

    width = D // H
    if line:
        half = width // Q
        wide = 256
        pieces = width // wide
        at_edge = jnp.logical_or(hh == 0, hh == 3)
        edge = jnp.where(hh < 2, 0, 3)
        near_mid = jnp.where(hh < 2, 1, 2)
        partner = jnp.where(at_edge, near_mid, edge)
        far = 3 - hh
        far_copies = []
        for i, w_hbm in enumerate((wk_hbm, wv_hbm)):
            far_copies.append(
                pltpu.make_async_remote_copy(
                    src_ref=w_hbm.at[
                        pl.ds(pl.multiple_of(far * width + qb * half, half), half), :
                    ],
                    dst_ref=far_w.at[
                        pl.ds(pl.multiple_of(qb * half, half), half), pl.ds(i * hd, hd)
                    ],
                    send_sem=far_send.at[i],
                    recv_sem=far_recv.at[i],
                    device_id=(ly, far, qb),
                    device_id_type=MESH,
                )
            )

        @pl.when(at_edge)
        def _():
            for copy in far_copies:
                copy.start()

    @pl.when(needed(me, qb))
    def _():
        for k in range(2):
            kv[k, me] = mine[:, k * hd : (k + 1) * hd]

    blank = jnp.zeros((r, hd), BF16)
    for d in range(n):

        @pl.when(jnp.logical_not(needed(d, qb)))
        def _(d=d):
            kv[0, d] = blank
            kv[1, d] = blank

        @pl.when(jnp.logical_not(needed(me, d % Q)))
        def _(d=d):
            rbuf[0, d] = blank
            rbuf[1, d] = blank

    docs_load.wait()
    docs = docs_ref[...].reshape(1, S)
    own_docs = docs[:, 0:R]
    for b in range(1, Q):
        own_docs = jnp.where(qb == b, docs[:, b * R : (b + 1) * R], own_docs)
    own_docs = jnp.concatenate([own_docs] * G, axis=1)
    key_docs = jnp.transpose(jnp.broadcast_to(docs, (128, S)))[:, 0:1]
    first_key = jnp.sum((key_docs < own_docs).astype(F32), axis=0, keepdims=True).astype(jnp.int32)
    position = qb * R + jnp.concatenate(
        [lax.broadcasted_iota(jnp.int32, (1, R), 1)] * G, axis=1
    )


    for load in loads[base:]:
        load.wait()

    def gathered(k):
        for peer in peers:

            @pl.when(needed(peer, qb))
            def _(peer=peer):
                gather_copy(k, peer, peer).wait_recv()

        if r % 16 == 0:
            kvf[k] = kv[k].reshape(S, hd)
        else:
            for d in range(n):
                kvf[k, d * r : (d + 1) * r, :] = kv[k, d]

    gathered(0)

    cols = G * R
    blocks = S // kb

    def run(body, carry):
        if blocks == 1:
            return body(0, carry)
        return lax.fori_loop(0, blocks, body, carry)

    def rows_of(j):
        return pl.ds(pl.multiple_of(j * kb, kb), kb) if blocks > 1 else pl.ds(0, kb)

    def scores(j, top):
        rows = rows_of(j)
        key_pos = j * kb + lax.broadcasted_iota(jnp.int32, (kb, cols), 0)
        visible = (key_pos >= first_key) & (key_pos <= position)
        s = lax.dot_general(kvf[0, rows, :], qf[...], NT, preferred_element_type=F32) * scaling
        s = jnp.where(visible, s, -1e30)
        st[rows, :] = s
        return jnp.maximum(top, jnp.max(s, axis=0, keepdims=True))

    top = run(scores, jnp.full((1, cols), -1e30, F32))

    def totals(j, total):
        rows = rows_of(j)
        p = jnp.exp(st[rows, :] - top)
        st[rows, :] = p
        return total + jnp.sum(p, axis=0, keepdims=True)

    zero_row = jnp.zeros((1, cols), F32)
    inverse = 1.0 / run(totals, zero_row)

    def keep(k, j, grad):
        grad = grad.astype(BF16)
        if blocks == 1:
            sbuf[k] = grad.reshape(n, r, hd)
        else:
            per = kb // r
            for i in range(per):
                sbuf[k, j * per + i] = grad[i * r : (i + 1) * r]

    def value_grads(j, carry):
        rows = rows_of(j)
        p = st[rows, :] * inverse
        st[rows, :] = p
        keep(1, j, jnp.dot(p.astype(BF16), gf[...], preferred_element_type=F32))
        return carry

    def reduce_copy(k, peer, slot):
        return pltpu.make_async_remote_copy(
            src_ref=sbuf.at[k, peer],
            dst_ref=rbuf.at[k, slot],
            send_sem=rs_send.at[k * n + peer],
            recv_sem=rs_recv.at[k * n + slot],
            device_id=place(peer),
            device_id_type=MESH,
        )

    def scatter(k):
        for peer in peers:

            @pl.when(needed(peer, qb))
            def _(peer=peer):
                reduce_copy(k, peer, me).start()

        @pl.when(needed(me, qb))
        def _():
            rbuf[k, me] = sbuf[k, me]

    run(value_grads, 0)
    scatter(1)
    gathered(1)

    def dots(j, dot):
        rows = rows_of(j)
        grad = lax.dot_general(kvf[1, rows, :], gf[...], NT, preferred_element_type=F32)
        dpt[rows, :] = grad
        return dot + jnp.sum(st[rows, :] * grad, axis=0, keepdims=True)

    delta = run(dots, zero_row)

    def key_grads(j, carry):
        rows = rows_of(j)
        ds = (st[rows, :] * (dpt[rows, :] - delta)).astype(BF16)
        ds16[rows, :] = ds
        keep(0, j, jnp.dot(ds, qf[...], preferred_element_type=F32) * scaling)
        return carry

    run(key_grads, 0)
    scatter(0)

    def query_grads(j, carry):
        rows = rows_of(j)
        return carry + lax.dot_general(
            ds16[rows, :], kvf[0, rows, :], TN, preferred_element_type=F32
        )

    dq = run(query_grads, jnp.zeros((cols, hd), F32)) * scaling
    for g in range(G):
        qg_ref[0, :, g * hd : (g + 1) * hd] = dq[g * R : (g + 1) * R].astype(BF16)

    for k in (1, 0):
        for peer in peers:

            @pl.when(needed(me, lax.rem(peer, Q)))
            def _(k=k, peer=peer):
                reduce_copy(k, peer, peer).wait_recv()

    halves = []
    for k in range(2):
        owned = rbuf[k, 0].astype(F32)
        for d in range(1, n):
            owned = owned + rbuf[k, d].astype(F32)
        halves.append(owned.astype(BF16))
    owned = jnp.concatenate(halves, axis=1)

    def part_of(head):
        rows = pl.ds(pl.multiple_of(head * width, width), width)
        return lax.dot_general(owned, w_v[rows, :], NT, preferred_element_type=F32)

    if line:
        own_kv[...] = owned

        def chunk_of(head, c):
            rows = pl.ds(pl.multiple_of(head * width + c * wide, wide), wide)
            return lax.dot_general(owned, w_v[rows, :], NT, preferred_element_type=F32)

        def stream(k, c, head):
            return pltpu.make_async_remote_copy(
                src_ref=zsend.at[k, c],
                dst_ref=zrecv.at[k, c],
                send_sem=z_send.at[k * pieces + c],
                recv_sem=z_recv.at[k * pieces + c],
                device_id=(ly, head, qb),
                device_id_type=MESH,
            )

        factor = pltpu.make_async_remote_copy(
            src_ref=own_kv,
            dst_ref=far_kv,
            send_sem=far_send.at[2],
            recv_sem=far_recv.at[2],
            device_id=(ly, far, qb),
            device_id_type=MESH,
        )
        first_head = jnp.where(at_edge, 3 - near_mid, edge)
        second_head = jnp.where(at_edge, near_mid, 3 - edge)

        @pl.when(at_edge)
        def _():
            factor.start()

        for c in range(pieces):
            zsend[0, c] = chunk_of(first_head, c).astype(BF16)
            stream(0, c, partner).start()
        for c in range(pieces):
            zsend[1, c] = chunk_of(second_head, c).astype(BF16)
            stream(1, c, second_head).start()

        @pl.when(jnp.logical_not(at_edge))
        def _():
            for c in range(pieces):
                mine2 = chunk_of(3 - hh, c)
                stream(0, c, partner).wait_recv()
                zsend[2, c] = (mine2 + zrecv[0, c].astype(F32)).astype(BF16)
                stream(2, c, 3 - hh).start()
            for c in range(pieces):
                total_c = chunk_of(hh, c)
                stream(1, c, second_head).wait_recv()
                total_c = total_c + zrecv[1, c].astype(F32)
                stream(2, c, 3 - hh).wait_recv()
                total_c = total_c + zrecv[2, c].astype(F32)
                ig_ref[:, c * wide : (c + 1) * wide] = total_c.astype(BF16)
            for c in range(pieces):
                stream(2, c, 3 - hh).wait_send()

        @pl.when(at_edge)
        def _():
            for copy in far_copies:
                copy.wait_recv()
            share = pl.ds(pl.multiple_of(qb * half, half), half)
            swap = pltpu.make_async_remote_copy(
                src_ref=far_w.at[share, :],
                dst_ref=far_w.at[share, :],
                send_sem=far_send.at[3],
                recv_sem=far_recv.at[3],
                device_id=(ly, hh, 1 - qb),
                device_id_type=MESH,
            )
            swap.start()
            other_share = pl.ds(pl.multiple_of((1 - qb) * half, half), half)
            arriving = pltpu.make_async_remote_copy(
                src_ref=far_w.at[share, :],
                dst_ref=far_w.at[other_share, :],
                send_sem=far_send.at[3],
                recv_sem=far_recv.at[3],
                device_id=(ly, hh, 1 - qb),
                device_id_type=MESH,
            )
            factor.wait_recv()
            arriving.wait_recv()
            for c in range(pieces):
                total_c = chunk_of(hh, c) + lax.dot_general(
                    far_kv[...],
                    far_w[c * wide : (c + 1) * wide, :],
                    NT,
                    preferred_element_type=F32,
                )
                stream(0, c, partner).wait_recv()
                total_c = total_c + zrecv[0, c].astype(F32)
                stream(1, c, second_head).wait_recv()
                total_c = total_c + zrecv[1, c].astype(F32)
                ig_ref[:, c * wide : (c + 1) * wide] = total_c.astype(BF16)
            for copy in far_copies:
                copy.wait_send()
            factor.wait_send()
            swap.wait_send()

        for c in range(pieces):
            stream(0, c, partner).wait_send()
            stream(1, c, second_head).wait_send()
    else:
        z_copies = []
        for o in range(1, H):
            other = heads[o - 1]
            zsend[o - 1] = part_of(other).astype(BF16)
            copy = pltpu.make_async_remote_copy(
                src_ref=zsend.at[o - 1],
                dst_ref=zrecv.at[o - 1],
                send_sem=z_send.at[o - 1],
                recv_sem=z_recv.at[o - 1],
                device_id=(ly, other, qb),
                device_id_type=MESH,
            )
            copy.start()
            z_copies.append(copy)
        result = part_of(hh)
        for o, copy in enumerate(z_copies):
            copy.wait_recv()
            result = result + zrecv[o].astype(F32)
        ig_ref[...] = result.astype(BF16)

        for copy in z_copies:
            copy.wait_send()

    for k in range(2):
        for peer in peers:

            @pl.when(needed(me, lax.rem(peer, Q)))
            def _(k=k, peer=peer):
                gather_copy(k, peer, me).wait_send()

            @pl.when(needed(peer, qb))
            def _(k=k, peer=peer):
                reduce_copy(k, peer, me).wait_send()


def write_kernel(qg_in, ig_in, qg_out, ig_out, sems):
    copies = [
        pltpu.make_async_copy(qg_in, qg_out, sems.at[0]),
        pltpu.make_async_copy(ig_in, ig_out, sems.at[1]),
    ]
    for copy in copies:
        copy.start()
    for copy in copies:
        copy.wait()


def solution(mesh):
    L, H, Q = mesh.shape["layer"], mesh.shape["head"], mesh.shape["qblk"]
    n = L * Q

    def local(inputs, key_weight, value_weight, queries, output_cotangent, documents):
        r, D = inputs.shape
        hd = key_weight.shape[1]
        _, R, wide = queries.shape
        G = wide // hd
        S = documents.shape[0]
        chunks = 4
        kb = min(S, 384)
        line = H == 4 and Q == 2 and (D // H) % 256 == 0
        sizes = (L, H, Q, r, R, S, D, hd, G, chunks, kb, line)
        width = D // H
        streams = (3, width // 256, r, 256) if line else (H - 1, r, width)
        sends = 3 * (width // 256) if line else H - 1
        far_rows = width if line else 16
        cols = G * R
        anywhere = pl.BlockSpec(memory_space=pl.ANY)
        vmem = pl.BlockSpec(memory_space=pltpu.VMEM)
        dma = pltpu.SemaphoreType.DMA
        query_grad, input_grad = pl.pallas_call(
            functools.partial(backward_kernel, sizes),
            out_shape=(
                pltpu.VMEM(queries.shape, BF16),
                pltpu.VMEM((r, D // H), BF16),
            ),
            in_specs=[anywhere] * 6,
            out_specs=(vmem, vmem),
            scratch_shapes=[
                pltpu.VMEM((r, D), BF16),
                pltpu.VMEM((D, 2 * hd), BF16),
                pltpu.VMEM((cols, hd), BF16),
                pltpu.VMEM((cols, hd), BF16),
                pltpu.VMEM((2, n, r, hd), BF16),
                pltpu.VMEM((2, S, hd), BF16),
                pltpu.VMEM((S, cols), F32),
                pltpu.VMEM((S, cols), F32),
                pltpu.VMEM((S, cols), BF16),
                pltpu.VMEM((2, n, r, hd), BF16),
                pltpu.VMEM((2, n, r, hd), BF16),
                pltpu.VMEM(streams, BF16),
                pltpu.VMEM(streams, BF16),
                pltpu.VMEM((far_rows, 2 * hd), BF16),
                pltpu.VMEM((r, 2 * hd), BF16),
                pltpu.VMEM((r, 2 * hd), BF16),
                pltpu.VMEM((2, r, hd), BF16),
                pltpu.VMEM((S,), jnp.int32),
                dma((2 + 2 * chunks + 2 * G,)),
                dma((2 * n,)),
                dma((2 * n,)),
                dma((2 * n,)),
                dma((2 * n,)),
                dma((sends,)),
                dma((sends,)),
                dma((4,)),
                dma((4,)),
            ],
            compiler_params=pltpu.CompilerParams(
                collective_id=0, has_side_effects=True, vmem_limit_bytes=60 * 1024 * 1024
            ),
        )(
            inputs,
            key_weight,
            value_weight,
            queries,
            output_cotangent,
            documents,
        )
        return pl.pallas_call(
            write_kernel,
            out_shape=(
                jax.ShapeDtypeStruct(query_grad.shape, BF16),
                jax.ShapeDtypeStruct(input_grad.shape, BF16),
            ),
            in_specs=[vmem] * 2,
            out_specs=(anywhere, anywhere),
            scratch_shapes=[dma((2,))],
            compiler_params=pltpu.CompilerParams(vmem_limit_bytes=1024 * 1024),
        )(query_grad, input_grad)

    placed = (
        P(("layer", "qblk"), None),
        P(None, "head"),
        P(None, "head"),
        P("layer", "qblk", "head"),
        P("layer", "qblk", "head"),
        P(),
    )
    return jax.shard_map(
        local,
        mesh=mesh,
        in_specs=placed,
        out_specs=(P("layer", "qblk", "head"), P(("layer", "qblk"), "head")),
        check_vma=False,
    )
```

profile of v0, /device:TPU:0, one launch (start us, length us, event | category | flops | bytes accessed | tf_op | source)
XLA Modules:
  0.0 24.3 jit_solution(16213377344930007153)
XLA Ops:
  0.6 22.9 %shard_map.77 = (bf16[1,192,640]{2,1,0:T(8,128)(2,1)S(1)}, bf16[48,1280]{1,0:T(8,128)(2,1)S(1)}) custom-call(bf16[48,5120]{1,0:T(8,128)(2,1)} %x_hbm.1, bf16[5120,128]{1,0:T(8,128)(2,1)} %wk_hbm.1, bf16[5120,128]{1,0:T(8,128)(2,1)} %wv_hbm.1, bf16[1,192,640]{2,1,0:T(8,128)(2,1)} %q_hbm.1, bf16[1,192,640]{2,1,0:T(8,128)(2,1)} %g_hbm.1, s32[384]{0:T(512)} %docs_hbm.1), custom_call_target="tpu_custom_call" | custom-call | tf_op jit(solution)/shard_map/pallas_call | solution.py:523
  23.6 0.7 %shard_map.78 = (bf16[1,192,640]{2,1,0:T(8,128)(2,1)}, bf16[48,1280]{1,0:T(8,128)(2,1)}) custom-call(bf16[1,192,640]{2,1,0:T(8,128)(2,1)S(1)} %get-tuple-element.4.qg_in, bf16[48,1280]{1,0:T(8,128)(2,1)S(1)} %get-tuple-element.5.ig_in), custom_call_target="tpu_custom_call" | custom-call | tf_op jit(solution)/shard_map/pallas_call | solution.py:571
where the time goes:
time: 24.5 us; the launch traced here: 24.3 us
  Pallas kernels  23.7 us (97%)
  between operations  0.64 us (3%)
    pallas_call x1, Pallas kernels, local(): pl.pallas_call(functools.partial(backward_kernel, sizes), out_shape=(pltp...  22.9 us
    pallas_call x1, Pallas kernels, local(): pl.pallas_call(write_kernel, out_shape=(jax.ShapeDtypeStruct(query_grad.s...  0.75 us

commit v1 on v0

--- a/solution.py
+++ b/solution.py
@@ -487,6 +487,15 @@
                 reduce_copy(k, peer, me).wait_send()
 
 
+def scoped_kernel(sizes, *refs):
+    L, H, Q, r, R, S, D, hd, G, chunks, kb, line = sizes
+    n = L * Q
+    sends = 3 * (D // H // 256) if line else H - 1
+    dma = pltpu.SemaphoreType.DMA
+    counts = [2 + 2 * chunks + 2 * G, 2 * n, 2 * n, 2 * n, 2 * n, sends, sends, 4, 4]
+    pl.run_scoped(lambda *sems: backward_kernel(sizes, *refs, *sems), *[dma((c,)) for c in counts])
+
+
 def write_kernel(qg_in, ig_in, qg_out, ig_out, sems):
     copies = [
         pltpu.make_async_copy(qg_in, qg_out, sems.at[0]),
@@ -514,14 +523,13 @@
         sizes = (L, H, Q, r, R, S, D, hd, G, chunks, kb, line)
         width = D // H
         streams = (3, width // 256, r, 256) if line else (H - 1, r, width)
-        sends = 3 * (width // 256) if line else H - 1
         far_rows = width if line else 16
         cols = G * R
         anywhere = pl.BlockSpec(memory_space=pl.ANY)
         vmem = pl.BlockSpec(memory_space=pltpu.VMEM)
         dma = pltpu.SemaphoreType.DMA
         query_grad, input_grad = pl.pallas_call(
-            functools.partial(backward_kernel, sizes),
+            functools.partial(scoped_kernel, sizes),
             out_shape=(
                 pltpu.VMEM(queries.shape, BF16),
                 pltpu.VMEM((r, D // H), BF16),
@@ -547,15 +555,6 @@
                 pltpu.VMEM((r, 2 * hd), BF16),
                 pltpu.VMEM((2, r, hd), BF16),
                 pltpu.VMEM((S,), jnp.int32),
-                dma((2 + 2 * chunks + 2 * G,)),
-                dma((2 * n,)),
-                dma((2 * n,)),
-                dma((2 * n,)),
-                dma((2 * n,)),
-                dma((sends,)),
-                dma((sends,)),
-                dma((4,)),
-                dma((4,)),
             ],
             compiler_params=pltpu.CompilerParams(
                 collective_id=0, has_side_effects=True, vmem_limit_bytes=60 * 1024 * 1024

time: 24.5 us -> 23.4 us (0.955)
  Pallas kernels: 23.7 us -> 22.6 us
    pallas_call x1, Pallas kernels: 22.9 us -> 21.8 us  [local(): pl.pallas_call(functools.partial(scoped_kernel, sizes), out_shape=(pltpu....]
where the time goes in v1:
time: 23.4 us; the launch traced here: 23.2 us
  Pallas kernels  22.6 us (97%)
  between operations  0.64 us (3%)
    pallas_call x1, Pallas kernels, local(): pl.pallas_call(functools.partial(scoped_kernel, sizes), out_shape=(pltpu....  21.8 us
    pallas_call x1, Pallas kernels, local(): pl.pallas_call(write_kernel, out_shape=(jax.ShapeDtypeStruct(query_grad.s...  0.75 us

profile of v1, /device:TPU:0, one launch (start us, length us, event | category | flops | bytes accessed | tf_op | source)
XLA Modules:
  0.0 23.2 jit_solution(13271918540647200150)
XLA Ops:
  0.6 21.8 %shard_map.77 = (bf16[1,192,640]{2,1,0:T(8,128)(2,1)S(1)}, bf16[48,1280]{1,0:T(8,128)(2,1)S(1)}) custom-call(bf16[48,5120]{1,0:T(8,128)(2,1)} %refs_0_.1, bf16[5120,128]{1,0:T(8,128)(2,1)} %refs_1_.1, bf16[5120,128]{1,0:T(8,128)(2,1)} %refs_2_.1, bf16[1,192,640]{2,1,0:T(8,128)(2,1)} %refs_3_.1, bf16[1,192,640]{2,1,0:T(8,128)(2,1)} %refs_4_.1, s32[384]{0:T(512)} %refs_5_.1), custom_call_target="tpu_custom_call" | custom-call | tf_op jit(solution)/shard_map/pallas_call | solution.py:531
  22.5 0.7 %shard_map.78 = (bf16[1,192,640]{2,1,0:T(8,128)(2,1)}, bf16[48,1280]{1,0:T(8,128)(2,1)}) custom-call(bf16[1,192,640]{2,1,0:T(8,128)(2,1)S(1)} %get-tuple-element.4.qg_in, bf16[48,1280]{1,0:T(8,128)(2,1)S(1)} %get-tuple-element.5.ig_in), custom_call_target="tpu_custom_call" | custom-call | tf_op jit(solution)/shard_map/pallas_call | solution.py:570

commit v2 on v1

v2 whole, which is shorter than its diff:
```python
import functools

import jax
import jax.numpy as jnp
from jax import lax
from jax.experimental import pallas as pl
from jax.experimental.pallas import tpu as pltpu
from jax.sharding import PartitionSpec as P

MESH = pl.DeviceIdType.MESH
NT = (((1,), (1,)), ((), ()))
TN = (((0,), (0,)), ((), ()))
F32 = jnp.float32
BF16 = jnp.bfloat16


def backward_kernel(
    sizes,
    x_hbm,
    wk_hbm,
    wv_hbm,
    q_hbm,
    g_hbm,
    docs_hbm,
    qg_ref,
    ig_ref,
    x_v,
    w_v,
    qf,
    gf,
    kv,
    kvf,
    st,
    dpt,
    ds16,
    acc_kv,
    sbuf,
    rbuf,
    zsend,
    zrecv,
    far_w,
    far_kv,
    own_kv,
    total,
    own_v,
    docs_ref,
    load_sem,
    ag_send,
    ag_recv,
    rs_send,
    rs_recv,
    z_send,
    z_recv,
    wz_send,
    wz_recv,
    wx_send,
    wx_recv,
    wt_send,
    wt_recv,
    kv_send,
    kv_recv,
):
    L, H, Q, r, R, S, D, hd, G, chunks, kb, line, band = sizes
    n = L * Q
    scaling = hd ** (-0.5)
    span = S // 2
    ly = lax.axis_index("layer")
    hh = lax.axis_index("head")
    qb = lax.axis_index("qblk")
    me = ly * Q + qb

    def needed(owner, block):
        above = owner * r < (block + 1) * R
        below = (owner + 1) * r - 1 >= block * R - span + 1
        return jnp.logical_and(above, below)

    def place(peer):
        return (peer // Q, hh, lax.rem(peer, Q))

    if L == 4 and Q == 2:
        row, col = ly // 2, lax.rem(ly, 2)
        far_layer = (1 - row) * 2 + 1 - col
        next_layers = [row * 2 + 1 - col, (1 - row) * 2 + col]
        peers = [far_layer * Q + qb, far_layer * Q + 1 - qb]
        peers += [layer * Q + qb for layer in next_layers]
        peers += [layer * Q + 1 - qb for layer in next_layers]
        peers += [ly * Q + 1 - qb]
    else:
        peers = [lax.rem(me + o, n) for o in range(1, n)]
    heads = [lax.rem(hh + o, H) for o in range(1, H)]

    barrier = pltpu.get_barrier_semaphore()
    for other in heads:
        pl.semaphore_signal(barrier, inc=1, device_id=(ly, other, qb), device_id_type=MESH)
    for peer in peers:
        pl.semaphore_signal(barrier, inc=1, device_id=place(peer), device_id_type=MESH)

    step = D // chunks
    loads = []
    for c in range(chunks):
        rows = pl.ds(c * step, step)
        loads.append(
            pltpu.make_async_copy(x_hbm.at[:, rows], x_v.at[:, rows], load_sem.at[3 * c])
        )
        loads.append(
            pltpu.make_async_copy(
                wk_hbm.at[rows, :], w_v.at[rows, pl.ds(0, hd)], load_sem.at[3 * c + 1]
            )
        )
        loads.append(
            pltpu.make_async_copy(
                wv_hbm.at[rows, :], w_v.at[rows, pl.ds(hd, hd)], load_sem.at[3 * c + 2]
            )
        )
    base = 3 * chunks
    docs_load = pltpu.make_async_copy(docs_hbm, docs_ref, load_sem.at[base + 2])
    docs_load.start()
    parts = R // band if band else 1
    tall = R // parts
    for i in range(parts):
        for g in range(G):
            cols = pl.ds(g * hd, hd)
            take = pl.ds(i * tall, tall)
            rows = pl.ds((i * G + g) * tall, tall)
            loads.append(
                pltpu.make_async_copy(q_hbm.at[0, take, cols], qf.at[rows, :], load_sem.at[base])
            )
            loads.append(
                pltpu.make_async_copy(
                    g_hbm.at[0, take, cols], gf.at[rows, :], load_sem.at[base + 1]
                )
            )
    for load in loads:
        load.start()

    acc = jnp.zeros((r, 2 * hd), F32)
    for c in range(chunks):
        for load in loads[3 * c : 3 * c + 3]:
            load.wait()
        acc = acc + jnp.dot(
            x_v[:, c * step : (c + 1) * step],
            w_v[c * step : (c + 1) * step, :],
            preferred_element_type=F32,
        )
    mine = acc.astype(BF16)
    for k in range(2):
        own_v[k] = mine[:, k * hd : (k + 1) * hd]
    pl.semaphore_wait(barrier, n - 1 + H - 1)

    def gather_copy(k, peer, slot):
        return pltpu.make_async_remote_copy(
            src_ref=own_v.at[k],
            dst_ref=kv.at[k, slot],
            send_sem=ag_send.at[k * n + peer],
            recv_sem=ag_recv.at[k * n + slot],
            device_id=place(peer),
            device_id_type=MESH,
        )

    for k in range(2):
        for peer in peers:

            @pl.when(needed(me, lax.rem(peer, Q)))
            def _(k=k, peer=peer):
                gather_copy(k, peer, me).start()

    width = D // H
    if line:
        half = width // Q
        piece = half // L
        wide = 256
        pieces = width // wide
        at_edge = jnp.logical_or(hh == 0, hh == 3)
        near = hh + 1 - 2 * lax.rem(hh, 2)
        second = lax.rem(hh + 2, 4)
        opposite = 3 - hh
        qb_rows = pl.ds(pl.multiple_of(qb * half, half), half)
        other_rows = pl.ds(pl.multiple_of((1 - qb) * half, half), half)

        column = lax.rem(ly, 2)
        spots = [ly, column, 2 + ly // 2]
        beside = [ly + 1 - 2 * column, lax.rem(ly + 2, L)]

        def piece_rows(first, spot):
            return pl.ds(pl.multiple_of(first + qb * half + spot * piece, piece), piece)

        def prefetch(way, head):
            return pltpu.make_async_remote_copy(
                src_ref=w_v.at[piece_rows(head * width, spots[way]), :],
                dst_ref=far_w.at[min(way, 1), piece_rows(0, spots[way]), :],
                send_sem=wz_send.at[way],
                recv_sem=wz_recv.at[way],
                device_id=(ly, head, qb),
                device_id_type=MESH,
            )

        def share(layer, source):
            return pltpu.make_async_remote_copy(
                src_ref=far_w.at[0, piece_rows(0, source), :],
                dst_ref=far_w.at[0, piece_rows(0, source), :],
                send_sem=wx_send.at[layer],
                recv_sem=wx_recv.at[source],
                device_id=(layer, hh, qb),
                device_id_type=MESH,
            )

        def swap(way, spot):
            return pltpu.make_async_remote_copy(
                src_ref=far_w.at[1, piece_rows(0, spot), :],
                dst_ref=far_w.at[1, piece_rows(0, spot), :],
                send_sem=wx_send.at[L + way],
                recv_sem=wx_recv.at[L + way],
                device_id=(beside[way], hh, qb),
                device_id_type=MESH,
            )

        def twin(slot, rows):
            return pltpu.make_async_remote_copy(
                src_ref=far_w.at[slot, rows, :],
                dst_ref=far_w.at[slot, rows, :],
                send_sem=wt_send.at[slot],
                recv_sem=wt_recv.at[slot],
                device_id=(ly, hh, 1 - qb),
                device_id_type=MESH,
            )

        other_layers = [lax.rem(ly + o, L) for o in range(1, L)]

        prefetch(0, second).start()

    @pl.when(needed(me, qb))
    def _():
        for k in range(2):
            kv[k, me] = mine[:, k * hd : (k + 1) * hd]

    blank = jnp.zeros((r, hd), BF16)
    for d in range(n):

        @pl.when(jnp.logical_not(needed(d, qb)))
        def _(d=d):
            kv[0, d] = blank
            kv[1, d] = blank

        @pl.when(jnp.logical_not(needed(me, d % Q)))
        def _(d=d):
            rbuf[0, d] = blank
            rbuf[1, d] = blank

    docs_load.wait()
    docs = docs_ref[...].reshape(1, S)
    own_docs = docs[:, 0:R]
    for b in range(1, Q):
        own_docs = jnp.where(qb == b, docs[:, b * R : (b + 1) * R], own_docs)
    key_docs = jnp.transpose(jnp.broadcast_to(docs, (128, S)))[:, 0:1]
    first_key = jnp.sum((key_docs < own_docs).astype(F32), axis=0, keepdims=True).astype(jnp.int32)
    position = qb * R + lax.broadcasted_iota(jnp.int32, (1, R), 1)
    if band:
        first_keys = []
        positions = []
        for i in range(parts):
            take = slice(i * tall, (i + 1) * tall)
            first_keys.append(jnp.concatenate([first_key[:, take]] * G, axis=1))
            positions.append(jnp.concatenate([position[:, take]] * G, axis=1))
    else:
        first_key = jnp.concatenate([first_key] * G, axis=1)
        position = jnp.concatenate([position] * G, axis=1)

    pltpu.make_async_copy(qf, qf, load_sem.at[base]).wait()
    pltpu.make_async_copy(gf, gf, load_sem.at[base + 1]).wait()

    def gathered(k):
        for peer in peers:

            @pl.when(needed(peer, qb))
            def _(peer=peer):
                gather_copy(k, peer, peer).wait_recv()

        if r % 16 == 0:
            kvf[k] = kv[k].reshape(S, hd)
        else:
            for d in range(n):
                kvf[k, d * r : (d + 1) * r, :] = kv[k, d]

    gathered(0)
    if line:

        @pl.when(at_edge)
        def _():
            prefetch(1, opposite).start()
            prefetch(2, opposite).start()


    def reduce_copy(k, peer, slot):
        return pltpu.make_async_remote_copy(
            src_ref=sbuf.at[k, peer],
            dst_ref=rbuf.at[k, slot],
            send_sem=rs_send.at[k * n + peer],
            recv_sem=rs_recv.at[k * n + slot],
            device_id=place(peer),
            device_id_type=MESH,
        )

    def scatter(k):
        for peer in peers:

            @pl.when(needed(peer, qb))
            def _(peer=peer):
                reduce_copy(k, peer, me).start()

        @pl.when(needed(me, qb))
        def _():
            rbuf[k, me] = sbuf[k, me]

    if band:
        high = span + tall
        wide_cols = G * tall
        starts = [
            pl.multiple_of(jnp.maximum(qb * R + i * tall - span, 0), tall) for i in range(parts)
        ]
        windows = [pl.ds(start, high) for start in starts]
        takes = [slice(i * wide_cols, (i + 1) * wide_cols) for i in range(parts)]

        def hand_over(k, factor):
            for d in range(n):
                grad = acc_kv[k, d * r : (d + 1) * r, :]
                sbuf[k, d] = (grad * factor if factor else grad).astype(BF16)

        acc_kv[...] = jnp.zeros(acc_kv.shape, F32)
        tops = []
        for i in range(parts):
            key_pos = starts[i] + lax.broadcasted_iota(jnp.int32, (high, wide_cols), 0)
            visible = (key_pos >= first_keys[i]) & (key_pos <= positions[i])
            s = lax.dot_general(
                kvf[0, windows[i], :], qf[takes[i], :], NT, preferred_element_type=F32
            )
            s = jnp.where(visible, s * scaling, -1e30)
            st[i] = s
            tops.append(jnp.max(s, axis=0, keepdims=True))
        for i in range(parts):
            p = jnp.exp(st[i] - tops[i])
            p = p * (1.0 / jnp.sum(p, axis=0, keepdims=True))
            st[i] = p
            acc_kv[1, windows[i], :] += jnp.dot(
                p.astype(BF16), gf[takes[i], :], preferred_element_type=F32
            )
        hand_over(1, None)
        scatter(1)
        gathered(1)
        for i in range(parts):
            grad = lax.dot_general(
                kvf[1, windows[i], :], gf[takes[i], :], NT, preferred_element_type=F32
            )
            p = st[i]
            delta = jnp.sum(p * grad, axis=0, keepdims=True)
            ds = (p * (grad - delta)).astype(BF16)
            ds16[i] = ds
            acc_kv[0, windows[i], :] += jnp.dot(ds, qf[takes[i], :], preferred_element_type=F32)
        hand_over(0, scaling)
        scatter(0)
        for i in range(parts):
            dq = scaling * lax.dot_general(
                ds16[i], kvf[0, windows[i], :], TN, preferred_element_type=F32
            )
            for g in range(G):
                qg_ref[0, i * tall : (i + 1) * tall, g * hd : (g + 1) * hd] = dq[
                    g * tall : (g + 1) * tall
                ].astype(BF16)
    else:
        cols = G * R
        blocks = S // kb

        def run(body, carry):
            if blocks == 1:
                return body(0, carry)
            return lax.fori_loop(0, blocks, body, carry)

        def rows_of(j):
            return pl.ds(pl.multiple_of(j * kb, kb), kb) if blocks > 1 else pl.ds(0, kb)

        def scores(j, top):
            rows = rows_of(j)
            key_pos = j * kb + lax.broadcasted_iota(jnp.int32, (kb, cols), 0)
            visible = (key_pos >= first_key) & (key_pos <= position)
            s = lax.dot_general(kvf[0, rows, :], qf[...], NT, preferred_element_type=F32) * scaling
            s = jnp.where(visible, s, -1e30)
            st[rows, :] = s
            return jnp.maximum(top, jnp.max(s, axis=0, keepdims=True))

        top = run(scores, jnp.full((1, cols), -1e30, F32))

        def totals(j, total):
            rows = rows_of(j)
            p = jnp.exp(st[rows, :] - top)
            st[rows, :] = p
            return total + jnp.sum(p, axis=0, keepdims=True)

        zero_row = jnp.zeros((1, cols), F32)
        inverse = 1.0 / run(totals, zero_row)

        def keep(k, j, grad):
            grad = grad.astype(BF16)
            if blocks == 1:
                sbuf[k] = grad.reshape(n, r, hd)
            else:
                per = kb // r
                for i in range(per):
                    sbuf[k, j * per + i] = grad[i * r : (i + 1) * r]

        def value_grads(j, carry):
            rows = rows_of(j)
            p = st[rows, :] * inverse
            st[rows, :] = p
            keep(1, j, jnp.dot(p.astype(BF16), gf[...], preferred_element_type=F32))
            return carry

        run(value_grads, 0)
        scatter(1)
        gathered(1)

        def dots(j, dot):
            rows = rows_of(j)
            grad = lax.dot_general(kvf[1, rows, :], gf[...], NT, preferred_element_type=F32)
            dpt[rows, :] = grad
            return dot + jnp.sum(st[rows, :] * grad, axis=0, keepdims=True)

        delta = run(dots, zero_row)

        def key_grads(j, carry):
            rows = rows_of(j)
            ds = (st[rows, :] * (dpt[rows, :] - delta)).astype(BF16)
            ds16[rows, :] = ds
            keep(0, j, jnp.dot(ds, qf[...], preferred_element_type=F32) * scaling)
            return carry

        run(key_grads, 0)
        scatter(0)

        def query_grads(j, carry):
            rows = rows_of(j)
            return carry + lax.dot_general(
                ds16[rows, :], kvf[0, rows, :], TN, preferred_element_type=F32
            )

        dq = run(query_grads, jnp.zeros((cols, hd), F32)) * scaling
        for g in range(G):
            qg_ref[0, :, g * hd : (g + 1) * hd] = dq[g * R : (g + 1) * R].astype(BF16)

    if line:
        prefetch(0, second).wait_recv()
        for layer in other_layers:
            share(layer, ly).start()

    for k in (1, 0):
        for peer in peers:

            @pl.when(needed(me, lax.rem(peer, Q)))
            def _(k=k, peer=peer):
                reduce_copy(k, peer, peer).wait_recv()

    halves = []
    for k in range(2):
        owned = rbuf[k, 0].astype(F32)
        for d in range(1, n):
            owned = owned + rbuf[k, d].astype(F32)
        halves.append(owned.astype(BF16))
    owned = jnp.concatenate(halves, axis=1)

    def part_of(head):
        rows = pl.ds(pl.multiple_of(head * width, width), width)
        return lax.dot_general(owned, w_v[rows, :], NT, preferred_element_type=F32)

    if line:
        own_kv[...] = owned

        def chunk_of(head, c):
            rows = pl.ds(pl.multiple_of(head * width + c * wide, wide), wide)
            return lax.dot_general(owned, w_v[rows, :], NT, preferred_element_type=F32)

        def far_chunk(slot, c):
            return lax.dot_general(
                far_kv[slot],
                far_w[slot, c * wide : (c + 1) * wide, :],
                NT,
                preferred_element_type=F32,
            )

        def factor(slot, head):
            return pltpu.make_async_remote_copy(
                src_ref=own_kv,
                dst_ref=far_kv.at[slot],
                send_sem=kv_send.at[slot],
                recv_sem=kv_recv.at[slot],
                device_id=(ly, head, qb),
                device_id_type=MESH,
            )

        def stream(k, c, head):
            return pltpu.make_async_remote_copy(
                src_ref=zsend.at[k, c],
                dst_ref=zrecv.at[k, c],
                send_sem=z_send.at[k * pieces + c],
                recv_sem=z_recv.at[k * pieces + c],
                device_id=(ly, head, qb),
                device_id_type=MESH,
            )

        @pl.when(at_edge)
        def _():
            factor(1, opposite).start()

        factor(0, second).start()

        @pl.when(jnp.logical_not(at_edge))
        def _():
            for c in range(pieces):
                zsend[1, c] = chunk_of(opposite, c).astype(BF16)
                stream(1, c, opposite).start()

        for c in range(pieces):
            zsend[0, c] = chunk_of(near, c).astype(BF16)
            stream(0, c, near).start()

        for c in range(pieces):
            total[:, c * wide : (c + 1) * wide] = chunk_of(hh, c)

        @pl.when(at_edge)
        def _():
            for way in (1, 2):
                prefetch(way, opposite).wait_recv()
                swap(way - 1, spots[way]).start()

        for layer in other_layers:
            share(layer, layer).wait_recv()
        twin(0, qb_rows).start()

        @pl.when(at_edge)
        def _():
            swap(0, 1 - column).wait_recv()
            swap(1, 3 - ly // 2).wait_recv()
            twin(1, qb_rows).start()

        factor(0, second).wait_recv()
        twin(0, other_rows).wait_recv()
        for c in range(pieces):
            total[:, c * wide : (c + 1) * wide] += far_chunk(0, c)

        @pl.when(at_edge)
        def _():
            factor(1, opposite).wait_recv()
            twin(1, other_rows).wait_recv()
            for c in range(pieces):
                total[:, c * wide : (c + 1) * wide] += far_chunk(1, c)

        @pl.when(jnp.logical_not(at_edge))
        def _():
            for c in range(pieces):
                stream(1, c, opposite).wait_recv()
                total[:, c * wide : (c + 1) * wide] += zrecv[1, c].astype(F32)

        for c in range(pieces):
            stream(0, c, near).wait_recv()
            cols_c = slice(c * wide, (c + 1) * wide)
            ig_ref[:, cols_c] = (total[:, cols_c] + zrecv[0, c].astype(F32)).astype(BF16)

        @pl.when(at_edge)
        def _():
            for way in (1, 2):
                prefetch(way, opposite).wait_send()
                swap(way - 1, spots[way]).wait_send()
            twin(1, qb_rows).wait_send()
            factor(1, opposite).wait_send()

        @pl.when(jnp.logical_not(at_edge))
        def _():
            for c in range(pieces):
                stream(1, c, opposite).wait_send()

        prefetch(0, second).wait_send()
        for layer in other_layers:
            share(layer, ly).wait_send()
        twin(0, qb_rows).wait_send()
        factor(0, second).wait_send()
        for c in range(pieces):
            stream(0, c, near).wait_send()
    else:
        z_copies = []
        for o in range(1, H):
            other = heads[o - 1]
            zsend[o - 1] = part_of(other).astype(BF16)
            copy = pltpu.make_async_remote_copy(
                src_ref=zsend.at[o - 1],
                dst_ref=zrecv.at[o - 1],
                send_sem=z_send.at[o - 1],
                recv_sem=z_recv.at[o - 1],
                device_id=(ly, other, qb),
                device_id_type=MESH,
            )
            copy.start()
            z_copies.append(copy)
        result = part_of(hh)
        for o, copy in enumerate(z_copies):
            copy.wait_recv()
            result = result + zrecv[o].astype(F32)
        ig_ref[...] = result.astype(BF16)

        for copy in z_copies:
            copy.wait_send()

    for k in range(2):
        for peer in peers:

            @pl.when(needed(me, lax.rem(peer, Q)))
            def _(k=k, peer=peer):
                gather_copy(k, peer, me).wait_send()

            @pl.when(needed(peer, qb))
            def _(k=k, peer=peer):
                reduce_copy(k, peer, me).wait_send()


def scoped_kernel(sizes, *refs):
    L, H, Q, r, R, S, D, hd, G, chunks, kb, line, band = sizes
    n = L * Q
    sends = 2 * (D // H // 256) if line else H - 1
    dma = pltpu.SemaphoreType.DMA
    counts = [3 + 3 * chunks, 2 * n, 2 * n, 2 * n, 2 * n, sends, sends]
    counts += [3, 3, 2 + L, 2 + L, 2, 2, 2, 2]
    pl.run_scoped(lambda *sems: backward_kernel(sizes, *refs, *sems), *[dma((c,)) for c in counts])


def write_kernel(qg_in, ig_in, qg_out, ig_out, sems):
    copies = [
        pltpu.make_async_copy(qg_in, qg_out, sems.at[0]),
        pltpu.make_async_copy(ig_in, ig_out, sems.at[1]),
    ]
    for copy in copies:
        copy.start()
    for copy in copies:
        copy.wait()


def solution(mesh):
    L, H, Q = mesh.shape["layer"], mesh.shape["head"], mesh.shape["qblk"]
    n = L * Q

    def local(inputs, key_weight, value_weight, queries, output_cotangent, documents):
        r, D = inputs.shape
        hd = key_weight.shape[1]
        _, R, wide = queries.shape
        G = wide // hd
        S = documents.shape[0]
        chunks = D // 1024 if D % 1024 == 0 else 4
        kb = min(S, 384)
        line_mesh = L == 4 and H == 4 and Q == 2
        band = r if line_mesh and S == 2 * R and R % r == 0 and r % 16 == 0 else 0
        line = line_mesh and (D // H) % 256 == 0
        sizes = (L, H, Q, r, R, S, D, hd, G, chunks, kb, line, band)
        width = D // H
        streams = (2, width // 256, r, 256) if line else (H - 1, r, width)
        far_rows = width if line else 16
        cols = G * R
        tile = (R // band, S // 2 + band, G * band) if band else (S, cols)
        anywhere = pl.BlockSpec(memory_space=pl.ANY)
        vmem = pl.BlockSpec(memory_space=pltpu.VMEM)
        dma = pltpu.SemaphoreType.DMA
        query_grad, input_grad = pl.pallas_call(
            functools.partial(scoped_kernel, sizes),
            out_shape=(
                pltpu.VMEM(queries.shape, BF16),
                pltpu.VMEM((r, D // H), BF16),
            ),
            in_specs=[anywhere] * 6,
            out_specs=(vmem, vmem),
            scratch_shapes=[
                pltpu.VMEM((r, D), BF16),
                pltpu.VMEM((D, 2 * hd), BF16),
                pltpu.VMEM((cols, hd), BF16),
                pltpu.VMEM((cols, hd), BF16),
                pltpu.VMEM((2, n, r, hd), BF16),
                pltpu.VMEM((2, S, hd), BF16),
                pltpu.VMEM(tile, F32),
                pltpu.VMEM(tile if not band else (8, 128), F32),
                pltpu.VMEM(tile, BF16),
                pltpu.VMEM((2, S, hd) if band else (2, 8, hd), F32),
                pltpu.VMEM((2, n, r, hd), BF16),
                pltpu.VMEM((2, n, r, hd), BF16),
                pltpu.VMEM(streams, BF16),
                pltpu.VMEM(streams, BF16),
                pltpu.VMEM((2, far_rows, 2 * hd), BF16),
                pltpu.VMEM((2, r, 2 * hd), BF16),
                pltpu.VMEM((r, 2 * hd), BF16),
                pltpu.VMEM((r, width), F32),
                pltpu.VMEM((2, r, hd), BF16),
                pltpu.VMEM((S,), jnp.int32),
            ],
            compiler_params=pltpu.CompilerParams(
                collective_id=0, has_side_effects=True, vmem_limit_bytes=60 * 1024 * 1024
            ),
        )(
            inputs,
            key_weight,
            value_weight,
            queries,
            output_cotangent,
            documents,
        )
        return pl.pallas_call(
            write_kernel,
            out_shape=(
                jax.ShapeDtypeStruct(query_grad.shape, BF16),
                jax.ShapeDtypeStruct(input_grad.shape, BF16),
            ),
            in_specs=[vmem] * 2,
            out_specs=(anywhere, anywhere),
            scratch_shapes=[dma((2,))],
            compiler_params=pltpu.CompilerParams(vmem_limit_bytes=1024 * 1024),
        )(query_grad, input_grad)

    placed = (
        P(("layer", "qblk"), None),
        P(None, "head"),
        P(None, "head"),
        P("layer", "qblk", "head"),
        P("layer", "qblk", "head"),
        P(),
    )
    return jax.shard_map(
        local,
        mesh=mesh,
        in_specs=placed,
        out_specs=(P("layer", "qblk", "head"), P(("layer", "qblk"), "head")),
        check_vma=False,
    )
```

time: 23.4 us -> 22.4 us (0.957)
  Pallas kernels: 22.6 us -> 21.4 us
    pallas_call x1, Pallas kernels: 21.8 us -> 20.6 us  [local(): pl.pallas_call(functools.partial(scoped_kernel, sizes), out_shape=(pltpu....]
where the time goes in v2:
time: 22.4 us; the launch traced here: 22 us
  Pallas kernels  21.4 us (96%)
  between operations  0.64 us (3%)
    pallas_call x1, Pallas kernels, local(): pl.pallas_call(functools.partial(scoped_kernel, sizes), out_shape=(pltpu....  20.6 us
    pallas_call x1, Pallas kernels, local(): pl.pallas_call(write_kernel, out_shape=(jax.ShapeDtypeStruct(query_grad.s...  0.75 us

profile of v2, /device:TPU:0, one launch (start us, length us, event | category | flops | bytes accessed | tf_op | source)
XLA Modules:
  0.0 22.0 jit_solution(15336504908633624224)
XLA Ops:
  0.6 20.6 %shard_map.77 = (bf16[1,192,640]{2,1,0:T(8,128)(2,1)S(1)}, bf16[48,1280]{1,0:T(8,128)(2,1)S(1)}) custom-call(bf16[48,5120]{1,0:T(8,128)(2,1)} %refs_0_.1, bf16[5120,128]{1,0:T(8,128)(2,1)} %refs_1_.1, bf16[5120,128]{1,0:T(8,128)(2,1)} %refs_2_.1, bf16[1,192,640]{2,1,0:T(8,128)(2,1)} %refs_3_.1, bf16[1,192,640]{2,1,0:T(8,128)(2,1)} %refs_4_.1, s32[384]{0:T(512)} %refs_5_.1), custom_call_target="tpu_custom_call" | custom-call | tf_op jit(solution)/shard_map/pallas_call | solution.py:666
  21.2 0.7 %shard_map.78 = (bf16[1,192,640]{2,1,0:T(8,128)(2,1)}, bf16[48,1280]{1,0:T(8,128)(2,1)}) custom-call(bf16[1,192,640]{2,1,0:T(8,128)(2,1)S(1)} %get-tuple-element.4.qg_in, bf16[48,1280]{1,0:T(8,128)(2,1)S(1)} %get-tuple-element.5.ig_in), custom_call_target="tpu_custom_call" | custom-call | tf_op jit(solution)/shard_map/pallas_call | solution.py:707

commit v3 on v2

--- a/solution.py
+++ b/solution.py
@@ -174,8 +174,6 @@
         near = hh + 1 - 2 * lax.rem(hh, 2)
         second = lax.rem(hh + 2, 4)
         opposite = 3 - hh
-        qb_rows = pl.ds(pl.multiple_of(qb * half, half), half)
-        other_rows = pl.ds(pl.multiple_of((1 - qb) * half, half), half)
 
         column = lax.rem(ly, 2)
         spots = [ly, column, 2 + ly // 2]
@@ -214,12 +212,13 @@
                 device_id_type=MESH,
             )
 
-        def twin(slot, rows):
+        def twin(slot, spot, side):
+            rows = pl.ds(pl.multiple_of(side * half + spot * piece, piece), piece)
             return pltpu.make_async_remote_copy(
                 src_ref=far_w.at[slot, rows, :],
                 dst_ref=far_w.at[slot, rows, :],
-                send_sem=wt_send.at[slot],
-                recv_sem=wt_recv.at[slot],
+                send_sem=wt_send.at[slot * L + spot],
+                recv_sem=wt_recv.at[slot * L + spot],
                 device_id=(ly, hh, 1 - qb),
                 device_id_type=MESH,
             )
@@ -446,9 +445,14 @@
             qg_ref[0, :, g * hd : (g + 1) * hd] = dq[g * R : (g + 1) * R].astype(BF16)
 
     if line:
-        prefetch(0, second).wait_recv()
-        for layer in other_layers:
-            share(layer, ly).start()
+
+        def start_sharing():
+            prefetch(0, second).wait_recv()
+            for layer in other_layers:
+                share(layer, ly).start()
+            twin(0, ly, qb).start()
+
+        pl.when(at_edge)(start_sharing)
 
     for k in (1, 0):
         for peer in peers:
@@ -512,6 +516,7 @@
 
         @pl.when(jnp.logical_not(at_edge))
         def _():
+            start_sharing()
             for c in range(pieces):
                 zsend[1, c] = chunk_of(opposite, c).astype(BF16)
                 stream(1, c, opposite).start()
@@ -528,26 +533,29 @@
             for way in (1, 2):
                 prefetch(way, opposite).wait_recv()
                 swap(way - 1, spots[way]).start()
+                twin(1, spots[way], qb).start()
 
         for layer in other_layers:
             share(layer, layer).wait_recv()
-        twin(0, qb_rows).start()
-
-        @pl.when(at_edge)
-        def _():
-            swap(0, 1 - column).wait_recv()
-            swap(1, 3 - ly // 2).wait_recv()
-            twin(1, qb_rows).start()
+            twin(0, layer, qb).start()
 
         factor(0, second).wait_recv()
-        twin(0, other_rows).wait_recv()
+        for spot in range(L):
+            twin(0, spot, 1 - qb).wait_recv()
         for c in range(pieces):
             total[:, c * wide : (c + 1) * wide] += far_chunk(0, c)
 
         @pl.when(at_edge)
         def _():
+            for way, spot in enumerate((1 - column, 3 - ly // 2)):
+                swap(way, spot).wait_recv()
+                twin(1, spot, qb).start()
+
+        @pl.when(at_edge)
+        def _():
             factor(1, opposite).wait_recv()
-            twin(1, other_rows).wait_recv()
+            for spot in range(L):
+                twin(1, spot, 1 - qb).wait_recv()
             for c in range(pieces):
                 total[:, c * wide : (c + 1) * wide] += far_chunk(1, c)
 
@@ -567,7 +575,8 @@
             for way in (1, 2):
                 prefetch(way, opposite).wait_send()
                 swap(way - 1, spots[way]).wait_send()
-            twin(1, qb_rows).wait_send()
+            for spot in range(L):
+                twin(1, spot, qb).wait_send()
             factor(1, opposite).wait_send()
 
         @pl.when(jnp.logical_not(at_edge))
@@ -578,7 +587,8 @@
         prefetch(0, second).wait_send()
         for layer in other_layers:
             share(layer, ly).wait_send()
-        twin(0, qb_rows).wait_send()
+        for spot in range(L):
+            twin(0, spot, qb).wait_send()
         factor(0, second).wait_send()
         for c in range(pieces):
             stream(0, c, near).wait_send()
@@ -624,7 +634,7 @@
     sends = 2 * (D // H // 256) if line else H - 1
     dma = pltpu.SemaphoreType.DMA
     counts = [3 + 3 * chunks, 2 * n, 2 * n, 2 * n, 2 * n, sends, sends]
-    counts += [3, 3, 2 + L, 2 + L, 2, 2, 2, 2]
+    counts += [3, 3, 2 + L, 2 + L, 2 * L, 2 * L, 2, 2]
     pl.run_scoped(lambda *sems: backward_kernel(sizes, *refs, *sems), *[dma((c,)) for c in counts])
 
 

time: 22.4 us -> 22.2 us (level); the launches traced: 22 us -> 22 us
  no operation moved by 1% of the time
where the time goes in v3:
time: 22.2 us; the launch traced here: 22 us
  Pallas kernels  21.4 us (96%)
  between operations  0.64 us (3%)
    pallas_call x1, Pallas kernels, local(): pl.pallas_call(functools.partial(scoped_kernel, sizes), out_shape=(pltpu....  20.6 us
    pallas_call x1, Pallas kernels, local(): pl.pallas_call(write_kernel, out_shape=(jax.ShapeDtypeStruct(query_grad.s...  0.75 us

profile of v3, /device:TPU:0, one launch (start us, length us, event | category | flops | bytes accessed | tf_op | source)
XLA Modules:
  0.0 22.0 jit_solution(7646431876084206328)
XLA Ops:
  0.6 20.6 %shard_map.77 = (bf16[1,192,640]{2,1,0:T(8,128)(2,1)S(1)}, bf16[48,1280]{1,0:T(8,128)(2,1)S(1)}) custom-call(bf16[48,5120]{1,0:T(8,128)(2,1)} %refs_0_.1, bf16[5120,128]{1,0:T(8,128)(2,1)} %refs_1_.1, bf16[5120,128]{1,0:T(8,128)(2,1)} %refs_2_.1, bf16[1,192,640]{2,1,0:T(8,128)(2,1)} %refs_3_.1, bf16[1,192,640]{2,1,0:T(8,128)(2,1)} %refs_4_.1, s32[384]{0:T(512)} %refs_5_.1), custom_call_target="tpu_custom_call" | custom-call | tf_op jit(solution)/shard_map/pallas_call | solution.py:676
  21.3 0.7 %shard_map.78 = (bf16[1,192,640]{2,1,0:T(8,128)(2,1)}, bf16[48,1280]{1,0:T(8,128)(2,1)}) custom-call(bf16[1,192,640]{2,1,0:T(8,128)(2,1)S(1)} %get-tuple-element.4.qg_in, bf16[48,1280]{1,0:T(8,128)(2,1)S(1)} %get-tuple-element.5.ig_in), custom_call_target="tpu_custom_call" | custom-call | tf_op jit(solution)/shard_map/pallas_call | solution.py:717

commit v4 on v3

--- a/solution.py
+++ b/solution.py
@@ -223,7 +223,7 @@
                 device_id_type=MESH,
             )
 
-        other_layers = [lax.rem(ly + o, L) for o in range(1, L)]
+        other_layers = [*beside, L - 1 - ly]
 
         prefetch(0, second).start()
 
@@ -525,15 +525,15 @@
             zsend[0, c] = chunk_of(near, c).astype(BF16)
             stream(0, c, near).start()
 
-        for c in range(pieces):
-            total[:, c * wide : (c + 1) * wide] = chunk_of(hh, c)
-
         @pl.when(at_edge)
         def _():
             for way in (1, 2):
                 prefetch(way, opposite).wait_recv()
                 swap(way - 1, spots[way]).start()
                 twin(1, spots[way], qb).start()
+
+        for c in range(pieces):
+            total[:, c * wide : (c + 1) * wide] = chunk_of(hh, c)
 
         for layer in other_layers:
             share(layer, layer).wait_recv()

time: 22.2 us -> 22.2 us (level)
  no operation moved by 1% of the time
where the time goes in v4:
time: 22.2 us; the launch traced here: 22 us
  Pallas kernels  21.4 us (96%)
  between operations  0.64 us (3%)
    pallas_call x1, Pallas kernels, local(): pl.pallas_call(functools.partial(scoped_kernel, sizes), out_shape=(pltpu....  20.6 us
    pallas_call x1, Pallas kernels, local(): pl.pallas_call(write_kernel, out_shape=(jax.ShapeDtypeStruct(query_grad.s...  0.75 us

profile of v4, /device:TPU:0, one launch (start us, length us, event | category | flops | bytes accessed | tf_op | source)
XLA Modules:
  0.0 22.0 jit_solution(3469405023737645681)
XLA Ops:
  0.6 20.6 %shard_map.77 = (bf16[1,192,640]{2,1,0:T(8,128)(2,1)S(1)}, bf16[48,1280]{1,0:T(8,128)(2,1)S(1)}) custom-call(bf16[48,5120]{1,0:T(8,128)(2,1)} %refs_0_.1, bf16[5120,128]{1,0:T(8,128)(2,1)} %refs_1_.1, bf16[5120,128]{1,0:T(8,128)(2,1)} %refs_2_.1, bf16[1,192,640]{2,1,0:T(8,128)(2,1)} %refs_3_.1, bf16[1,192,640]{2,1,0:T(8,128)(2,1)} %refs_4_.1, s32[384]{0:T(512)} %refs_5_.1), custom_call_target="tpu_custom_call" | custom-call | tf_op jit(solution)/shard_map/pallas_call | solution.py:676
  21.3 0.7 %shard_map.78 = (bf16[1,192,640]{2,1,0:T(8,128)(2,1)}, bf16[48,1280]{1,0:T(8,128)(2,1)}) custom-call(bf16[1,192,640]{2,1,0:T(8,128)(2,1)S(1)} %get-tuple-element.4.qg_in, bf16[48,1280]{1,0:T(8,128)(2,1)S(1)} %get-tuple-element.5.ig_in), custom_call_target="tpu_custom_call" | custom-call | tf_op jit(solution)/shard_map/pallas_call | solution.py:717
